TPU v7x, 512 devices: a whole 4x8x8 slice. The times are simulated.
512 devices in a mesh: gx: 16 (over z, core), gy: 32 (over y, x).
Axes of the slice: x: 4, y: 8, z: 8, core: 2. Of those that a mesh axis runs over, the one named last changes fastest.
Arguments:
- positions: float32 [3, 16, 32, 4096], P(None, 'gx', 'gy'), may hold values from 0 to 2
- velocities: float32 [3, 16, 32, 4096], P(None, 'gx', 'gy'), may hold values from -6 to 6
- mass: float32 [16, 32, 4096], P('gx', 'gy'), may hold values from 0.05 to 0.3
- stiffness: float32 [16, 32, 4096], P('gx', 'gy'), may hold values from 0.5 to 8
- counts: int32 [16, 32, 32], P('gx', 'gy'), may hold values from 32 to 128
- pairs: int32 [65536, 2], P(('gx', 'gy')), may hold values from 0 to 16383, as said below
- pair_count: int32 [512], P(('gx', 'gy')), may hold values from 32 to 128, as said below
Outputs:
- new_positions: float32 [3, 16, 32, 4096], P(None, 'gx', 'gy')
- new_velocities: float32 [3, 16, 32, 4096], P(None, 'gx', 'gy')
- density: float32 [16, 32, 4096], P('gx', 'gy')
Inputs may be any that keep to these rules, and one draw needn't show every extreme that they name: `pairs`: box d's list is rows d * 128 to (d + 1) * 128 - 1, box d being (d // 32, d % 32). Its first 32 rows pair each of the box's own tiles with itself, in order. In every other row the first tile lies in a box with the same gy index and a gx index at most one away, the second tile in a box with the same gx index and a gy index at most one away. Rows may repeat. `pair_count`: some box has 128 live rows in every draw.
All inputs are finite; a program needn't handle non-finite values.
Results may differ from a plain program's by a relative error of at most 0.0001.
Values sent between devices are 32-bit elements; how exact they have to be, the bound alone decides.
A program may use at most 64 MiB of HBM per device.

v0:
```python
import functools
import math

import jax
import jax.numpy as jnp
from jax import lax
from jax.experimental import pallas as pl
from jax.experimental.pallas import tpu as pltpu
from jax.sharding import PartitionSpec as P

kernel_norm = 21.0 / (16.0 * math.pi)
viscosity = 0.1
time_step = 0.02
rest_density = 1.0

MESH = pl.DeviceIdType.MESH
OWN = 2
BOXES = 5
BESIDE = (0, 1, 3, 4)
KDEPTH = 24
FEATURES = 16
UNROLL = 16
FORCE_UNROLL = 32

f32, bf16 = jnp.float32, jnp.bfloat16


def split_in(value, parts):
    pieces = []
    for _ in range(parts):
        piece = value.astype(bf16)
        pieces.append(piece)
        value = value - piece.astype(f32)
    return pieces


def dot_nn(a, b):
    return lax.dot_general(a, b, (((1,), (0,)), ((), ())), preferred_element_type=f32)


def dot_nt(a, b):
    return lax.dot_general(a, b, (((1,), (1,)), ((), ())), preferred_element_type=f32)


def kernel(
    gx, gy, tiles, size, rows,
    pos_h, vel_h, mass_h, stiff_h, counts_h, pairs_h, live_s,
    points_out, speeds_out, density_out,
    pos, mass, counts, pairs_v, in_sem,
    pm, vs, side_a, side_b, mass_rows, feats, squares, weights, falls, slope,
    row_density, row_force, picks, table_v, table_s, table_sem,
    dens_part, dens_recv, dens_total, force_part, force_recv, send_sem, recv_sem,
):
    my_x, my_y = lax.axis_index("gx"), lax.axis_index("gy")
    where_to = {
        0: (my_x - 1, my_y),
        1: (my_x, my_y - 1),
        3: (my_x, my_y + 1),
        4: (my_x + 1, my_y),
    }
    there = {0: my_x > 0, 1: my_y > 0, 3: my_y < gy - 1, 4: my_x < gx - 1}
    all_tiles = BOXES * tiles
    plane_step, force_step = all_tiles + 1, 2 * rows + 1

    barrier = pltpu.get_barrier_semaphore()
    for b in BESIDE:

        @pl.when(there[b])
        def _(b=b):
            pl.semaphore_signal(barrier, inc=1, device_id=where_to[b], device_id_type=MESH)


    inputs = (
        (pos_h, pos),
        (mass_h, mass),
        (counts_h, counts),
        (pairs_h, pairs_v),
        (vel_h, vs.at[OWN, 0:3]),
        (stiff_h, vs.at[OWN, 3]),
    )
    loads = [pltpu.make_async_copy(a, b, in_sem.at[k]) for k, (a, b) in enumerate(inputs)]
    for load in loads:
        load.start()

    for load in loads[0:3]:
        load.wait()
    row_at = lax.broadcasted_iota(jnp.int32, (tiles, tiles), 0)
    column_at = lax.broadcasted_iota(jnp.int32, (tiles, tiles), 1)
    count = jnp.sum(
        jnp.where(row_at == column_at, counts[...].astype(f32), 0.0), axis=1, keepdims=True
    )
    lane = lax.broadcasted_iota(jnp.int32, (tiles, size), 1).astype(f32)
    for c in range(3):
        pm[OWN, c] = 0.5 * (pos[c] - 1.0)
    pm[OWN, 3] = jnp.where(lane < count, mass[...], 0.0)

    pl.semaphore_wait(barrier, sum(there[b].astype(jnp.int32) for b in BESIDE))

    def copy_to(stage, b, source, target):
        return pltpu.make_async_remote_copy(
            src_ref=source,
            dst_ref=target.at[4 - b],
            send_sem=send_sem.at[stage, b],
            recv_sem=recv_sem.at[stage, 4 - b],
            device_id=where_to[b],
            device_id_type=MESH,
        )

    def send_to(stage, b, source, target):
        @pl.when(there[b])
        def _():
            copy_to(stage, b, source, target).start()

    def exchange(stage, source_of, target):
        for b in BESIDE:
            send_to(stage, b, source_of(b), target)
        return stage, source_of, target

    def arrived(stage, b, target):
        @pl.when(there[b])
        def _():
            pltpu.make_async_remote_copy(
                src_ref=target.at[b],
                dst_ref=target.at[b],
                send_sem=send_sem.at[stage, b],
                recv_sem=recv_sem.at[stage, b],
                device_id=where_to[b],
                device_id_type=MESH,
            ).wait_recv()

    sent = []
    sent.append(exchange(0, lambda b: pm.at[OWN], pm))

    def at_plane(ref, plane, b):
        return ref.at[pl.ds(plane * plane_step + b * tiles, tiles)]

    def distance_planes(b):
        ones = jnp.ones((tiles, size), f32)
        norm = jnp.zeros((tiles, size), f32)
        planes_a, planes_b = [], []
        for c in range(3):
            h = pm[b, c]
            norm = norm + h * h
            h1, h2, h3 = (p.astype(f32) for p in split_in(h, 3))
            planes_a += [-2.0 * v for v in (h1, h1, h2, h2, h1, h3)]
            planes_b += [h1, h2, h1, h2, h3, h1]
        n_parts = [p.astype(f32) for p in split_in(norm, 3)]
        planes_a += n_parts + [ones] * 3
        planes_b += [ones] * 3 + n_parts
        if b in (0, OWN, 4):
            for k, value in enumerate(planes_a):
                at_plane(side_a, k, b)[...] = value
        if b in (1, OWN, 3):
            for k, value in enumerate(planes_b):
                at_plane(side_b, k, b)[...] = value
        for k, value in enumerate(split_in(pm[b, 3], 2)):
            at_plane(mass_rows, k, b)[...] = value.astype(f32)

    distance_planes(OWN)
    row_density[pl.ds(rows, tiles)] = jnp.zeros((tiles, size), f32)
    for f in range(12):
        row_force[pl.ds(f * force_step + rows, tiles)] = jnp.zeros((tiles, size), f32)

    loads[3].wait()
    first = pairs_v[0:1, :]
    second = pairs_v[1:2, :]
    row_index = lax.broadcasted_iota(jnp.int32, (1, rows), 1)
    live = row_index < live_s[0]

    first_tile = (OWN + 2 * (lax.div(first, gy * tiles) - my_x)) * tiles + lax.rem(first, tiles)
    second_tile = (OWN + lax.rem(lax.div(second, tiles), gy) - my_y) * tiles + lax.rem(second, tiles)
    to_first = jnp.where(live, first_tile, -1)
    to_second = jnp.where(live & (first != second), second_tile, -1)
    tile_at = lax.broadcasted_iota(jnp.int32, (all_tiles, rows), 0)
    picks[:, 0:rows] = jnp.where(tile_at == to_first, 1.0, 0.0).astype(bf16)
    picks[:, rows : 2 * rows] = jnp.where(tile_at == to_second, 1.0, 0.0).astype(bf16)
    table_v[0:1] = jnp.clip(first_tile, 0, all_tiles - 1)
    table_v[1:2] = jnp.clip(second_tile, 0, all_tiles - 1)
    table_copy = pltpu.make_async_copy(table_v, table_s, table_sem)
    table_copy.start()

    def own_tiles(r):
        return OWN * tiles + r, OWN * tiles + r

    def listed_tiles(r):
        return table_s[0, r], table_s[1, r]

    def tile_rows(ref, tile, count):
        return ref[pl.ds(tile, count, stride=plane_step), :].astype(bf16)

    def twice(value):
        return jnp.concatenate([value, value], axis=1)

    def side_by_side(value):
        return jnp.concatenate([value[0:size], value[size : 2 * size]], axis=1)

    def distances(u, t1, t2):
        a = tile_rows(side_a, t1, KDEPTH)
        b = tile_rows(side_b, t2, KDEPTH)
        squares[u] = lax.dot_general(a, b, (((0,), (0,)), ((), ())), preferred_element_type=f32)

    def weigh(r, u):
        square = jnp.maximum(squares[u], 1e-13)
        fall = jnp.maximum(1.0 - square * lax.rsqrt(square), 0.0)
        fall2 = fall * fall
        falls[r] = fall
        weight_hi, weight_lo = split_in(fall2 * fall2 * (1.25 - fall), 2)
        weights[u, 0:size] = weight_hi
        weights[u, size : 2 * size] = weight_lo

    def add_up(r, u, t1, t2, cross):
        both = weights[u]
        got = dot_nt(twice(tile_rows(mass_rows, t2, 8)), side_by_side(both))
        row_density[pl.ds(r, 1)] = got[0:1] + got[1:2]
        if cross:
            got = dot_nn(twice(tile_rows(mass_rows, t1, 8)), both)
            row_density[pl.ds(rows + r, 1)] = got[0:1] + got[1:2]

    def density_rows(start, end, tiles_of, cross):
        for u in range(UNROLL):
            distances(u, *tiles_of(start + u))

        def turn(step, carry):
            for u in range(UNROLL):
                r = start + step * UNROLL + u
                before = jnp.maximum(r - UNROLL, start)
                spare = jnp.where(step == 0, 2 * rows + u, before)
                add_up(spare, u, *tiles_of(before), cross)
                weigh(r, u)
                distances(u, *tiles_of(jnp.minimum(r + UNROLL, end - 1)))
            return carry

        lax.fori_loop(0, (end - start) // UNROLL, turn, 0)
        for u in range(UNROLL):
            r = end - UNROLL + u
            add_up(r, u, *tiles_of(r), cross)

    def slopes(start, end):
        def turn(step, carry):
            for u in range(4):
                r = start + step * 4 + u
                fall = falls[r]
                slope_hi, slope_lo = split_in(fall * fall * fall, 2)
                slope[r, 0:size] = slope_hi
                slope[r, size : 2 * size] = slope_lo
            return carry

        lax.fori_loop(0, (end - start) // 4, turn, 0)

    def force_row(r, t1, t2, cross):
        both = slope[r]
        got = dot_nt(twice(tile_rows(feats, t2, 2 * FEATURES)), side_by_side(both))
        row_force[pl.ds(r, FEATURES, stride=force_step), :] = got[0:FEATURES] + got[FEATURES:]
        if cross:
            got = dot_nn(twice(tile_rows(feats, t1, 2 * FEATURES)), both)
            row_force[pl.ds(rows + r, FEATURES, stride=force_step), :] = (
                got[0:FEATURES] + got[FEATURES:]
            )

    def force_rows(start, end, tiles_of, cross):
        def turn(step, carry):
            for u in range(FORCE_UNROLL):
                r = start + step * FORCE_UNROLL + u
                force_row(r, *tiles_of(r), cross)
            return carry

        lax.fori_loop(0, (end - start) // FORCE_UNROLL, turn, 0)

    density_rows(0, tiles, own_tiles, False)
    table_copy.wait()
    for b in BESIDE:
        arrived(0, b, pm)
        distance_planes(b)
    for load in loads[4:6]:
        load.wait()
    sent.append(exchange(1, lambda b: vs.at[OWN], vs))
    density_rows(tiles, rows, listed_tiles, True)

    chosen = picks[...]
    total = jnp.zeros((all_tiles, size), f32)
    for part in split_in(row_density[0 : 2 * rows], 3):
        total = total + dot_nn(chosen, part)
    dens_part[...] = ((4.0 * kernel_norm) * total).reshape(BOXES, tiles, size)
    sent.append(exchange(2, lambda b: dens_part.at[b], dens_recv))
    slopes(0, rows // 2)
    density = dens_part[OWN]
    for b in BESIDE:
        arrived(2, b, dens_recv)
        density = density + jnp.where(there[b], dens_recv[b], 0.0)
    dens_total[OWN] = density
    density_out[...] = density
    sent.append(exchange(3, lambda b: dens_total.at[OWN], dens_total))

    def pressures(b):
        density = dens_total[b]
        scale = density + 1.0 - jnp.where(pm[b, 3] > 0.0, 1.0, 0.0)
        inverse = 1.0 / scale
        press = vs[b, 3] * (density - rest_density) * inverse * inverse
        return press, inverse

    def force_planes(b):
        press, inverse = pressures(b)
        m = pm[b, 3]
        mp, mq = m * press, m * inverse
        values = [m] + [m * pm[b, c] for c in range(3)]
        values += [mp] + [mp * pm[b, c] for c in range(3)]
        values += [mq] + [mq * vs[b, c] for c in range(3)]
        for k, value in enumerate(values):
            for part, piece in enumerate(split_in(value, 2)):
                at_plane(feats, part * FEATURES + k, b)[...] = piece.astype(f32)

    slopes(rows // 2, rows)
    force_planes(OWN)
    force_rows(0, tiles, own_tiles, False)
    for b in BESIDE:
        arrived(1, b, vs)
        arrived(3, b, dens_total)
        force_planes(b)
    force_rows(tiles, rows, listed_tiles, True)

    sums = []
    for f in range(0, 12, 2):
        pair = [split_in(row_force[pl.ds((f + k) * force_step, 2 * rows)], 2) for k in range(2)]
        total = jnp.zeros((all_tiles, 2 * size), f32)
        for part in range(2):
            total = total + dot_nn(
                chosen, jnp.concatenate([pair[0][part], pair[1][part]], axis=1)
            )
        sums += [total[:, 0:size], total[:, size:]]
    sent.append((4, lambda b: force_part.at[b], force_recv))
    for b in BESIDE + (OWN,):
        press, inverse = pressures(b)
        s = [v[b * tiles : (b + 1) * tiles] for v in sums]
        for c in range(3):
            h, v = pm[b, c], vs[b, c]
            push = press * (h * s[0] - s[1 + c]) + h * s[4] - s[5 + c]
            drag = inverse * (v * s[8] - s[9 + c])
            force_part[b, c] = (5.0 * kernel_norm) * (2.0 * push - (2.0 * viscosity) * drag)
        if b != OWN:
            send_to(4, b, force_part.at[b], force_recv)
    accel = force_part[OWN]
    for b in BESIDE:
        arrived(4, b, force_recv)
        accel = accel + jnp.where(there[b], force_recv[b], 0.0)
    accel = accel * jnp.where(pm[OWN, 3] > 0.0, 1.0, 0.0)[None]
    new_speeds = vs[OWN, 0:3] + time_step * accel
    speeds_out[...] = new_speeds
    points_out[...] = pos[...] + time_step * new_speeds

    for stage, source_of, target in sent:
        for b in BESIDE:

            @pl.when(there[b])
            def _(b=b):
                copy_to(stage, b, source_of(b), target).wait_send()


def store_kernel(points, speeds, density, points_out, speeds_out, density_out, sem):
    pairs = ((points, points_out), (speeds, speeds_out), (density, density_out))
    stores = [pltpu.make_async_copy(a, b, sem.at[k]) for k, (a, b) in enumerate(pairs)]
    for store in stores:
        store.start()
    for store in stores:
        store.wait()


def body(gx, gy, positions, velocities, mass, stiffness, counts, pairs, pair_count):
    tiles = counts.shape[2]
    size = positions.shape[3] // tiles
    rows = pairs.shape[0]
    all_tiles = BOXES * tiles
    points = positions.reshape(3, tiles, size)
    speeds = velocities.reshape(3, tiles, size)
    turned = pairs.T
    vmem = pl.BlockSpec(memory_space=pltpu.VMEM)
    hbm = pl.BlockSpec(memory_space=pltpu.HBM)
    shapes = (
        jax.ShapeDtypeStruct((3, tiles, size), f32),
        jax.ShapeDtypeStruct((3, tiles, size), f32),
        jax.ShapeDtypeStruct((tiles, size), f32),
    )
    results = pl.pallas_call(
        functools.partial(kernel, gx, gy, tiles, size, rows),
        out_shape=shapes,
        in_specs=[hbm] * 6 + [pl.BlockSpec(memory_space=pltpu.SMEM)],
        out_specs=(vmem,) * 3,
        scratch_shapes=[
            pltpu.VMEM((3, tiles, size), f32),
            pltpu.VMEM((tiles, size), f32),
            pltpu.VMEM((1, tiles), jnp.int32),
            pltpu.VMEM((2, rows), jnp.int32),
            pltpu.SemaphoreType.DMA((6,)),
            pltpu.VMEM((BOXES, 4, tiles, size), f32),
            pltpu.VMEM((BOXES, 4, tiles, size), f32),
            pltpu.VMEM((KDEPTH * (all_tiles + 1), size), f32),
            pltpu.VMEM((KDEPTH * (all_tiles + 1), size), f32),
            pltpu.VMEM((8 * (all_tiles + 1), size), f32),
            pltpu.VMEM((2 * FEATURES * (all_tiles + 1), size), f32),
            pltpu.VMEM((UNROLL, size, size), f32),
            pltpu.VMEM((UNROLL, 2 * size, size), bf16),
            pltpu.VMEM((rows, size, size), f32),
            pltpu.VMEM((rows, 2 * size, size), bf16),
            pltpu.VMEM((3 * rows + 16, size), f32),
            pltpu.VMEM((FEATURES * (2 * rows + 1), size), f32),
            pltpu.VMEM((all_tiles, 2 * rows), bf16),
            pltpu.VMEM((2, rows), jnp.int32),
            pltpu.SMEM((2, rows), jnp.int32),
            pltpu.SemaphoreType.DMA,
            pltpu.VMEM((BOXES, tiles, size), f32),
            pltpu.VMEM((BOXES, tiles, size), f32),
            pltpu.VMEM((BOXES, tiles, size), f32),
            pltpu.VMEM((BOXES, 3, tiles, size), f32),
            pltpu.VMEM((BOXES, 3, tiles, size), f32),
            pltpu.SemaphoreType.DMA((5, BOXES)),
            pltpu.SemaphoreType.DMA((5, BOXES)),
        ],
        compiler_params=pltpu.CompilerParams(collective_id=0, has_side_effects=True, vmem_limit_bytes=40 << 20),
        name="sph_step",
    )(
        *(
            pltpu.with_memory_space_constraint(value, pltpu.HBM)
            for value in (
                points,
                speeds,
                mass.reshape(tiles, size),
                stiffness.reshape(tiles, size),
                counts.reshape(1, tiles),
                turned,
            )
        ),
        pair_count,
    )
    new_points, new_speeds, density = pl.pallas_call(
        store_kernel,
        out_shape=shapes,
        in_specs=[vmem] * 3,
        out_specs=(hbm,) * 3,
        scratch_shapes=[pltpu.SemaphoreType.DMA((3,))],
        compiler_params=pltpu.CompilerParams(vmem_limit_bytes=1 << 20),
        name="sph_store",
    )(*results)
    return (
        new_points.reshape(positions.shape),
        new_speeds.reshape(velocities.shape),
        density.reshape(mass.shape),
    )


def solution(mesh):
    placed = (
        P(None, "gx", "gy", None),
        P(None, "gx", "gy", None),
        P("gx", "gy", None),
        P("gx", "gy", None),
        P("gx", "gy", None),
        P(("gx", "gy"), None),
        P(("gx", "gy")),
    )
    return jax.shard_map(
        functools.partial(body, mesh.shape["gx"], mesh.shape["gy"]),
        mesh=mesh,
        in_specs=placed,
        out_specs=(P(None, "gx", "gy", None), P(None, "gx", "gy", None), P("gx", "gy", None)),
        check_vma=False,
    )
```

profile of v0, /device:TPU:225, one launch (start us, length us, event | category | flops | bytes accessed | tf_op | source)
XLA Modules:
  0.0 34.0 jit_solution(15487177248590655970)
XLA Ops:
  1.3 32.0 %sph_step.1 = (f32[3,32,128]{2,1,0:T(8,128)S(1)}, f32[3,32,128]{2,1,0:T(8,128)S(1)}, f32[32,128]{1,0:T(8,128)S(1)}) custom-call(f32[3,32,128]{2,1,0:T(8,128)} %bitcast.9, f32[3,32,128]{2,1,0:T(8,128)} %bitcast.10, f32[32,128]{1,0:T(8,128)} %bitcast.11, f32[32,128]{1,0:T(8,128)} %bitcast.12, s32[1,32]{1,0:T(1,128)} %bitcast.14, s32[2,128]{1,0:T(2,128)} %bitcast.13, ...), custom_call_target="tpu_custom_call" | custom-call | tf_op jit(solution)/shard_map/sph_step/pallas_call | solution.py:382
  33.3 0.7 %sph_store.1 = (f32[3,32,128]{2,1,0:T(8,128)}, f32[3,32,128]{2,1,0:T(8,128)}, f32[32,128]{1,0:T(8,128)}) custom-call(f32[3,32,128]{2,1,0:T(8,128)S(1)} %get-tuple-element.9.points, f32[3,32,128]{2,1,0:T(8,128)S(1)} %get-tuple-element.10.speeds, f32[32,128]{1,0:T(8,128)S(1)} %get-tuple-element.11.density), custom_call_target="tpu_custom_call" | custom-call | tf_op jit(solution)/shard_map/sph_store/pallas_call | solution.py:433
where the time goes:
time: 34.2 us; the launch traced here: 34 us
  Pallas kernels  32.7 us (96%)
  between operations  1.29 us (4%)
    pallas_call x1, Pallas kernels, body(): pl.pallas_call(functools.partial(kernel, gx, gy, tiles, size, rows), out_...  32 us

commit v1 on v0

--- a/solution.py
+++ b/solution.py
@@ -16,7 +16,8 @@
 MESH = pl.DeviceIdType.MESH
 OWN = 2
 BOXES = 5
-BESIDE = (0, 1, 3, 4)
+BESIDE = (1, 3, 0, 4)
+INWARD = (0, 4, 1, 3)
 KDEPTH = 24
 FEATURES = 16
 UNROLL = 16
@@ -48,7 +49,7 @@
     points_out, speeds_out, density_out,
     pos, mass, counts, pairs_v, in_sem,
     pm, vs, side_a, side_b, mass_rows, feats, squares, weights, falls, slope,
-    row_density, row_force, picks, table_v, table_s, table_sem,
+    row_density, force_high, force_low, picks, table_v, table_s, table_sem,
     dens_part, dens_recv, dens_total, force_part, force_recv, send_sem, recv_sem,
 ):
     my_x, my_y = lax.axis_index("gx"), lax.axis_index("gy")
@@ -60,7 +61,7 @@
     }
     there = {0: my_x > 0, 1: my_y > 0, 3: my_y < gy - 1, 4: my_x < gx - 1}
     all_tiles = BOXES * tiles
-    plane_step, force_step = all_tiles + 1, 2 * rows + 1
+    plane_step, force_step = all_tiles + 1, 2 * rows + tiles + 1
 
     barrier = pltpu.get_barrier_semaphore()
     for b in BESIDE:
@@ -156,16 +157,13 @@
         for k, value in enumerate(split_in(pm[b, 3], 2)):
             at_plane(mass_rows, k, b)[...] = value.astype(f32)
 
-    distance_planes(OWN)
-    row_density[pl.ds(rows, tiles)] = jnp.zeros((tiles, size), f32)
-    for f in range(12):
-        row_force[pl.ds(f * force_step + rows, tiles)] = jnp.zeros((tiles, size), f32)
-
+    for start in (0, rows):
+        row_density[pl.ds(start, tiles)] = jnp.zeros((tiles, size), f32)
     loads[3].wait()
     first = pairs_v[0:1, :]
     second = pairs_v[1:2, :]
     row_index = lax.broadcasted_iota(jnp.int32, (1, rows), 1)
-    live = row_index < live_s[0]
+    live = (row_index < live_s[0]) & (row_index >= tiles)
 
     first_tile = (OWN + 2 * (lax.div(first, gy * tiles) - my_x)) * tiles + lax.rem(first, tiles)
     second_tile = (OWN + lax.rem(lax.div(second, tiles), gy) - my_y) * tiles + lax.rem(second, tiles)
@@ -178,6 +176,7 @@
     table_v[1:2] = jnp.clip(second_tile, 0, all_tiles - 1)
     table_copy = pltpu.make_async_copy(table_v, table_s, table_sem)
     table_copy.start()
+    distance_planes(OWN)
 
     def own_tiles(r):
         return OWN * tiles + r, OWN * tiles + r
@@ -194,14 +193,24 @@
     def side_by_side(value):
         return jnp.concatenate([value[0:size], value[size : 2 * size]], axis=1)
 
-    def distances(u, t1, t2):
-        a = tile_rows(side_a, t1, KDEPTH)
-        b = tile_rows(side_b, t2, KDEPTH)
-        squares[u] = lax.dot_general(a, b, (((0,), (0,)), ((), ())), preferred_element_type=f32)
+    def distances(u, one, two):
+        def stacked(ref, tile):
+            return ref[pl.ds(tile, KDEPTH, stride=plane_step), :]
+
+        a = jnp.concatenate([stacked(side_a, one[0]), stacked(side_a, two[0])], axis=0)
+        none = jnp.zeros((KDEPTH, size), f32)
+        left = jnp.concatenate([stacked(side_b, one[1]), none], axis=0)
+        right = jnp.concatenate([none, stacked(side_b, two[1])], axis=0)
+        b = jnp.concatenate([left.astype(bf16), right.astype(bf16)], axis=1)
+        both = lax.dot_general(
+            a.astype(bf16), b, (((0,), (0,)), ((), ())), preferred_element_type=f32
+        )
+        squares[u] = both[:, 0:size]
+        squares[u + 1] = both[:, size:]
 
     def weigh(r, u):
-        square = jnp.maximum(squares[u], 1e-13)
-        fall = jnp.maximum(1.0 - square * lax.rsqrt(square), 0.0)
+        square = lax.clamp(1e-13, squares[u], 1.0)
+        fall = 1.0 - square * lax.rsqrt(square)
         fall2 = fall * fall
         falls[r] = fall
         weight_hi, weight_lo = split_in(fall2 * fall2 * (1.25 - fall), 2)
@@ -211,23 +220,25 @@
     def add_up(r, u, t1, t2, cross):
         both = weights[u]
         got = dot_nt(twice(tile_rows(mass_rows, t2, 8)), side_by_side(both))
-        row_density[pl.ds(r, 1)] = got[0:1] + got[1:2]
+        row_density[pl.ds(r if cross else 2 * rows + r, 1)] = got[0:1] + got[1:2]
         if cross:
             got = dot_nn(twice(tile_rows(mass_rows, t1, 8)), both)
             row_density[pl.ds(rows + r, 1)] = got[0:1] + got[1:2]
 
     def density_rows(start, end, tiles_of, cross):
-        for u in range(UNROLL):
-            distances(u, *tiles_of(start + u))
+        for u in range(0, UNROLL, 2):
+            distances(u, tiles_of(start + u), tiles_of(start + u + 1))
 
         def turn(step, carry):
             for u in range(UNROLL):
                 r = start + step * UNROLL + u
                 before = jnp.maximum(r - UNROLL, start)
-                spare = jnp.where(step == 0, 2 * rows + u, before)
+                spare = jnp.where(step == 0, (2 * rows if cross else 0) + tiles + u, before)
                 add_up(spare, u, *tiles_of(before), cross)
                 weigh(r, u)
-                distances(u, *tiles_of(jnp.minimum(r + UNROLL, end - 1)))
+                if u % 2:
+                    ahead = jnp.minimum(r + UNROLL, end - 1)
+                    distances(u - 1, tiles_of(ahead - 1), tiles_of(ahead))
             return carry
 
         lax.fori_loop(0, (end - start) // UNROLL, turn, 0)
@@ -247,28 +258,30 @@
 
         lax.fori_loop(0, (end - start) // 4, turn, 0)
 
+    def keep_sums(row, got):
+        value = got[0:FEATURES] + got[FEATURES:]
+        high, low = (piece.astype(f32) for piece in split_in(value, 2))
+        force_high[pl.ds(row, FEATURES, stride=force_step), :] = high
+        force_low[pl.ds(row, FEATURES, stride=force_step), :] = low
+
     def force_row(r, t1, t2, cross):
         both = slope[r]
         got = dot_nt(twice(tile_rows(feats, t2, 2 * FEATURES)), side_by_side(both))
-        row_force[pl.ds(r, FEATURES, stride=force_step), :] = got[0:FEATURES] + got[FEATURES:]
+        keep_sums(r if cross else 2 * rows + r, got)
         if cross:
-            got = dot_nn(twice(tile_rows(feats, t1, 2 * FEATURES)), both)
-            row_force[pl.ds(rows + r, FEATURES, stride=force_step), :] = (
-                got[0:FEATURES] + got[FEATURES:]
-            )
-
-    def force_rows(start, end, tiles_of, cross):
+            keep_sums(rows + r, dot_nn(twice(tile_rows(feats, t1, 2 * FEATURES)), both))
+
+    def force_rows(start, end, tiles_of, cross, unroll=FORCE_UNROLL):
         def turn(step, carry):
-            for u in range(FORCE_UNROLL):
-                r = start + step * FORCE_UNROLL + u
+            for u in range(unroll):
+                r = start + step * unroll + u
                 force_row(r, *tiles_of(r), cross)
             return carry
 
-        lax.fori_loop(0, (end - start) // FORCE_UNROLL, turn, 0)
-
-    density_rows(0, tiles, own_tiles, False)
+        lax.fori_loop(0, (end - start) // unroll, turn, 0)
+
     table_copy.wait()
-    for b in BESIDE:
+    for b in INWARD:
         arrived(0, b, pm)
         distance_planes(b)
     for load in loads[4:6]:
@@ -282,9 +295,14 @@
         total = total + dot_nn(chosen, part)
     dens_part[...] = ((4.0 * kernel_norm) * total).reshape(BOXES, tiles, size)
     sent.append(exchange(2, lambda b: dens_part.at[b], dens_recv))
+    density_rows(0, tiles, own_tiles, False)
     slopes(0, rows // 2)
-    density = dens_part[OWN]
-    for b in BESIDE:
+    for ref in (force_high, force_low):
+        for f in range(12):
+            for start in (0, rows):
+                ref[pl.ds(f * force_step + start, tiles)] = jnp.zeros((tiles, size), f32)
+    density = dens_part[OWN] + (4.0 * kernel_norm) * row_density[2 * rows : 2 * rows + tiles]
+    for b in INWARD:
         arrived(2, b, dens_recv)
         density = density + jnp.where(there[b], dens_recv[b], 0.0)
     dens_total[OWN] = density
@@ -312,25 +330,27 @@
     slopes(rows // 2, rows)
     force_planes(OWN)
     force_rows(0, tiles, own_tiles, False)
-    for b in BESIDE:
+    for b in INWARD:
         arrived(1, b, vs)
         arrived(3, b, dens_total)
         force_planes(b)
-    force_rows(tiles, rows, listed_tiles, True)
+    force_rows(tiles, rows, listed_tiles, True, 48)
 
     sums = []
     for f in range(0, 12, 2):
-        pair = [split_in(row_force[pl.ds((f + k) * force_step, 2 * rows)], 2) for k in range(2)]
         total = jnp.zeros((all_tiles, 2 * size), f32)
-        for part in range(2):
-            total = total + dot_nn(
-                chosen, jnp.concatenate([pair[0][part], pair[1][part]], axis=1)
-            )
+        for ref in (force_high, force_low):
+            pair = [ref[pl.ds((f + k) * force_step, 2 * rows)].astype(bf16) for k in range(2)]
+            total = total + dot_nn(chosen, jnp.concatenate(pair, axis=1))
         sums += [total[:, 0:size], total[:, size:]]
     sent.append((4, lambda b: force_part.at[b], force_recv))
     for b in BESIDE + (OWN,):
         press, inverse = pressures(b)
         s = [v[b * tiles : (b + 1) * tiles] for v in sums]
+        if b == OWN:
+            for f in range(12):
+                own = pl.ds(f * force_step + 2 * rows, tiles)
+                s[f] = s[f] + force_high[own] + force_low[own]
         for c in range(3):
             h, v = pm[b, c], vs[b, c]
             push = press * (h * s[0] - s[1 + c]) + h * s[4] - s[5 + c]
@@ -339,7 +359,7 @@
         if b != OWN:
             send_to(4, b, force_part.at[b], force_recv)
     accel = force_part[OWN]
-    for b in BESIDE:
+    for b in INWARD:
         arrived(4, b, force_recv)
         accel = accel + jnp.where(there[b], force_recv[b], 0.0)
     accel = accel * jnp.where(pm[OWN, 3] > 0.0, 1.0, 0.0)[None]
@@ -400,8 +420,9 @@
             pltpu.VMEM((UNROLL, 2 * size, size), bf16),
             pltpu.VMEM((rows, size, size), f32),
             pltpu.VMEM((rows, 2 * size, size), bf16),
-            pltpu.VMEM((3 * rows + 16, size), f32),
-            pltpu.VMEM((FEATURES * (2 * rows + 1), size), f32),
+            pltpu.VMEM((3 * rows + 2 * tiles + 16, size), f32),
+            pltpu.VMEM((FEATURES * (2 * rows + tiles + 1), size), f32),
+            pltpu.VMEM((FEATURES * (2 * rows + tiles + 1), size), f32),
             pltpu.VMEM((all_tiles, 2 * rows), bf16),
             pltpu.VMEM((2, rows), jnp.int32),
             pltpu.SMEM((2, rows), jnp.int32),

time: 34.2 us -> 33.8 us (0.988)
  Pallas kernels: 32.7 us -> 32.3 us
    pallas_call x1, Pallas kernels: 32 us -> 31.7 us  [body(): pl.pallas_call(functools.partial(kernel, gx, gy, tiles, size, rows), out_...]
where the time goes in v1:
time: 33.8 us; the launch traced here: 33.6 us
  Pallas kernels  32.3 us (96%)
  between operations  1.29 us (4%)
    pallas_call x1, Pallas kernels, body(): pl.pallas_call(functools.partial(kernel, gx, gy, tiles, size, rows), out_...  31.7 us

profile of v1, /device:TPU:225, one launch (start us, length us, event | category | flops | bytes accessed | tf_op | source)
XLA Modules:
  0.0 33.6 jit_solution(12513710292974048840)
XLA Ops:
  1.3 31.7 %sph_step.1 = (f32[3,32,128]{2,1,0:T(8,128)S(1)}, f32[3,32,128]{2,1,0:T(8,128)S(1)}, f32[32,128]{1,0:T(8,128)S(1)}) custom-call(f32[3,32,128]{2,1,0:T(8,128)} %bitcast.9, f32[3,32,128]{2,1,0:T(8,128)} %bitcast.10, f32[32,128]{1,0:T(8,128)} %bitcast.11, f32[32,128]{1,0:T(8,128)} %bitcast.12, s32[1,32]{1,0:T(1,128)} %bitcast.14, s32[2,128]{1,0:T(2,128)} %bitcast.13, ...), custom_call_target="tpu_custom_call" | custom-call | tf_op jit(solution)/shard_map/sph_step/pallas_call | solution.py:402
  32.9 0.7 %sph_store.1 = (f32[3,32,128]{2,1,0:T(8,128)}, f32[3,32,128]{2,1,0:T(8,128)}, f32[32,128]{1,0:T(8,128)}) custom-call(f32[3,32,128]{2,1,0:T(8,128)S(1)} %get-tuple-element.9.points, f32[3,32,128]{2,1,0:T(8,128)S(1)} %get-tuple-element.10.speeds, f32[32,128]{1,0:T(8,128)S(1)} %get-tuple-element.11.density), custom_call_target="tpu_custom_call" | custom-call | tf_op jit(solution)/shard_map/sph_store/pallas_call | solution.py:454

commit v2 on v1

--- a/solution.py
+++ b/solution.py
@@ -280,6 +280,8 @@
 
         lax.fori_loop(0, (end - start) // unroll, turn, 0)
 
+    density_rows(0, tiles, own_tiles, False)
+    slopes(0, tiles)
     table_copy.wait()
     for b in INWARD:
         arrived(0, b, pm)
@@ -295,8 +297,7 @@
         total = total + dot_nn(chosen, part)
     dens_part[...] = ((4.0 * kernel_norm) * total).reshape(BOXES, tiles, size)
     sent.append(exchange(2, lambda b: dens_part.at[b], dens_recv))
-    density_rows(0, tiles, own_tiles, False)
-    slopes(0, rows // 2)
+    slopes(tiles, 3 * rows // 4)
     for ref in (force_high, force_low):
         for f in range(12):
             for start in (0, rows):
@@ -327,7 +328,7 @@
             for part, piece in enumerate(split_in(value, 2)):
                 at_plane(feats, part * FEATURES + k, b)[...] = piece.astype(f32)
 
-    slopes(rows // 2, rows)
+    slopes(3 * rows // 4, rows)
     force_planes(OWN)
     force_rows(0, tiles, own_tiles, False)
     for b in INWARD:

time: 33.8 us -> 33.8 us (level)
  no operation moved by 1% of the time
where the time goes in v2:
time: 33.8 us; the launch traced here: 33.6 us
  Pallas kernels  32.3 us (96%)
  between operations  1.29 us (4%)
    pallas_call x1, Pallas kernels, body(): pl.pallas_call(functools.partial(kernel, gx, gy, tiles, size, rows), out_...  31.7 us

profile of v2, /device:TPU:225, one launch (start us, length us, event | category | flops | bytes accessed | tf_op | source)
XLA Modules:
  0.0 33.6 jit_solution(16237214848765663665)
XLA Ops:
  1.3 31.7 %sph_step.1 = (f32[3,32,128]{2,1,0:T(8,128)S(1)}, f32[3,32,128]{2,1,0:T(8,128)S(1)}, f32[32,128]{1,0:T(8,128)S(1)}) custom-call(f32[3,32,128]{2,1,0:T(8,128)} %bitcast.9, f32[3,32,128]{2,1,0:T(8,128)} %bitcast.10, f32[32,128]{1,0:T(8,128)} %bitcast.11, f32[32,128]{1,0:T(8,128)} %bitcast.12, s32[1,32]{1,0:T(1,128)} %bitcast.14, s32[2,128]{1,0:T(2,128)} %bitcast.13, ...), custom_call_target="tpu_custom_call" | custom-call | tf_op jit(solution)/shard_map/sph_step/pallas_call | solution.py:403
  33.0 0.7 %sph_store.1 = (f32[3,32,128]{2,1,0:T(8,128)}, f32[3,32,128]{2,1,0:T(8,128)}, f32[32,128]{1,0:T(8,128)}) custom-call(f32[3,32,128]{2,1,0:T(8,128)S(1)} %get-tuple-element.9.points, f32[3,32,128]{2,1,0:T(8,128)S(1)} %get-tuple-element.10.speeds, f32[32,128]{1,0:T(8,128)S(1)} %get-tuple-element.11.density), custom_call_target="tpu_custom_call" | custom-call | tf_op jit(solution)/shard_map/sph_store/pallas_call | solution.py:455

commit v3 on v2

--- a/solution.py
+++ b/solution.py
@@ -100,7 +100,7 @@
     def copy_to(stage, b, source, target):
         return pltpu.make_async_remote_copy(
             src_ref=source,
-            dst_ref=target.at[4 - b],
+            dst_ref=target(4 - b),
             send_sem=send_sem.at[stage, b],
             recv_sem=recv_sem.at[stage, 4 - b],
             device_id=where_to[b],
@@ -121,16 +121,26 @@
         @pl.when(there[b])
         def _():
             pltpu.make_async_remote_copy(
-                src_ref=target.at[b],
-                dst_ref=target.at[b],
+                src_ref=target(b),
+                dst_ref=target(b),
                 send_sem=send_sem.at[stage, b],
                 recv_sem=recv_sem.at[stage, b],
                 device_id=where_to[b],
                 device_id_type=MESH,
             ).wait_recv()
 
+    def slot(ref):
+        return lambda b: ref.at[b]
+
+    def pos_of(b):
+        return pm.at[b, 0:3]
+
+    def mass_of(b):
+        return pm.at[b, 3]
+
     sent = []
-    sent.append(exchange(0, lambda b: pm.at[OWN], pm))
+    sent.append(exchange(0, lambda b: pos_of(OWN), pos_of))
+    sent.append(exchange(5, lambda b: mass_of(OWN), mass_of))
 
     def at_plane(ref, plane, b):
         return ref.at[pl.ds(plane * plane_step + b * tiles, tiles)]
@@ -154,6 +164,8 @@
         if b in (1, OWN, 3):
             for k, value in enumerate(planes_b):
                 at_plane(side_b, k, b)[...] = value
+
+    def mass_planes(b):
         for k, value in enumerate(split_in(pm[b, 3], 2)):
             at_plane(mass_rows, k, b)[...] = value.astype(f32)
 
@@ -177,6 +189,7 @@
     table_copy = pltpu.make_async_copy(table_v, table_s, table_sem)
     table_copy.start()
     distance_planes(OWN)
+    mass_planes(OWN)
 
     def own_tiles(r):
         return OWN * tiles + r, OWN * tiles + r
@@ -284,11 +297,14 @@
     slopes(0, tiles)
     table_copy.wait()
     for b in INWARD:
-        arrived(0, b, pm)
+        arrived(0, b, pos_of)
         distance_planes(b)
+    for b in INWARD:
+        arrived(5, b, mass_of)
+        mass_planes(b)
     for load in loads[4:6]:
         load.wait()
-    sent.append(exchange(1, lambda b: vs.at[OWN], vs))
+    sent.append(exchange(1, lambda b: vs.at[OWN], slot(vs)))
     density_rows(tiles, rows, listed_tiles, True)
 
     chosen = picks[...]
@@ -296,7 +312,7 @@
     for part in split_in(row_density[0 : 2 * rows], 3):
         total = total + dot_nn(chosen, part)
     dens_part[...] = ((4.0 * kernel_norm) * total).reshape(BOXES, tiles, size)
-    sent.append(exchange(2, lambda b: dens_part.at[b], dens_recv))
+    sent.append(exchange(2, lambda b: dens_part.at[b], slot(dens_recv)))
     slopes(tiles, 3 * rows // 4)
     for ref in (force_high, force_low):
         for f in range(12):
@@ -304,11 +320,11 @@
                 ref[pl.ds(f * force_step + start, tiles)] = jnp.zeros((tiles, size), f32)
     density = dens_part[OWN] + (4.0 * kernel_norm) * row_density[2 * rows : 2 * rows + tiles]
     for b in INWARD:
-        arrived(2, b, dens_recv)
+        arrived(2, b, slot(dens_recv))
         density = density + jnp.where(there[b], dens_recv[b], 0.0)
     dens_total[OWN] = density
     density_out[...] = density
-    sent.append(exchange(3, lambda b: dens_total.at[OWN], dens_total))
+    sent.append(exchange(3, lambda b: dens_total.at[OWN], slot(dens_total)))
 
     def pressures(b):
         density = dens_total[b]
@@ -332,8 +348,8 @@
     force_planes(OWN)
     force_rows(0, tiles, own_tiles, False)
     for b in INWARD:
-        arrived(1, b, vs)
-        arrived(3, b, dens_total)
+        arrived(1, b, slot(vs))
+        arrived(3, b, slot(dens_total))
         force_planes(b)
     force_rows(tiles, rows, listed_tiles, True, 48)
 
@@ -344,7 +360,7 @@
             pair = [ref[pl.ds((f + k) * force_step, 2 * rows)].astype(bf16) for k in range(2)]
             total = total + dot_nn(chosen, jnp.concatenate(pair, axis=1))
         sums += [total[:, 0:size], total[:, size:]]
-    sent.append((4, lambda b: force_part.at[b], force_recv))
+    sent.append((4, lambda b: force_part.at[b], slot(force_recv)))
     for b in BESIDE + (OWN,):
         press, inverse = pressures(b)
         s = [v[b * tiles : (b + 1) * tiles] for v in sums]
@@ -358,10 +374,10 @@
             drag = inverse * (v * s[8] - s[9 + c])
             force_part[b, c] = (5.0 * kernel_norm) * (2.0 * push - (2.0 * viscosity) * drag)
         if b != OWN:
-            send_to(4, b, force_part.at[b], force_recv)
+            send_to(4, b, force_part.at[b], slot(force_recv))
     accel = force_part[OWN]
     for b in INWARD:
-        arrived(4, b, force_recv)
+        arrived(4, b, slot(force_recv))
         accel = accel + jnp.where(there[b], force_recv[b], 0.0)
     accel = accel * jnp.where(pm[OWN, 3] > 0.0, 1.0, 0.0)[None]
     new_speeds = vs[OWN, 0:3] + time_step * accel
@@ -433,8 +449,8 @@
             pltpu.VMEM((BOXES, tiles, size), f32),
             pltpu.VMEM((BOXES, 3, tiles, size), f32),
             pltpu.VMEM((BOXES, 3, tiles, size), f32),
-            pltpu.SemaphoreType.DMA((5, BOXES)),
-            pltpu.SemaphoreType.DMA((5, BOXES)),
+            pltpu.SemaphoreType.DMA((6, BOXES)),
+            pltpu.SemaphoreType.DMA((6, BOXES)),
         ],
         compiler_params=pltpu.CompilerParams(collective_id=0, has_side_effects=True, vmem_limit_bytes=40 << 20),
         name="sph_step",

time: 33.8 us -> 33.8 us (level)
  no operation moved by 1% of the time
where the time goes in v3:
time: 33.8 us; the launch traced here: 33.7 us
  Pallas kernels  32.4 us (96%)
  between operations  1.29 us (4%)
    pallas_call x1, Pallas kernels, body(): pl.pallas_call(functools.partial(kernel, gx, gy, tiles, size, rows), out_...  31.7 us

profile of v3, /device:TPU:225, one launch (start us, length us, event | category | flops | bytes accessed | tf_op | source)
XLA Modules:
  0.0 33.7 jit_solution(3235690004290443673)
XLA Ops:
  1.3 31.7 %sph_step.1 = (f32[3,32,128]{2,1,0:T(8,128)S(1)}, f32[3,32,128]{2,1,0:T(8,128)S(1)}, f32[32,128]{1,0:T(8,128)S(1)}) custom-call(f32[3,32,128]{2,1,0:T(8,128)} %bitcast.9, f32[3,32,128]{2,1,0:T(8,128)} %bitcast.10, f32[32,128]{1,0:T(8,128)} %bitcast.11, f32[32,128]{1,0:T(8,128)} %bitcast.12, s32[1,32]{1,0:T(1,128)} %bitcast.14, s32[2,128]{1,0:T(2,128)} %bitcast.13, ...), custom_call_target="tpu_custom_call" | custom-call | tf_op jit(solution)/shard_map/sph_step/pallas_call | solution.py:419
  33.0 0.7 %sph_store.1 = (f32[3,32,128]{2,1,0:T(8,128)}, f32[3,32,128]{2,1,0:T(8,128)}, f32[32,128]{1,0:T(8,128)}) custom-call(f32[3,32,128]{2,1,0:T(8,128)S(1)} %get-tuple-element.9.points, f32[3,32,128]{2,1,0:T(8,128)S(1)} %get-tuple-element.10.speeds, f32[32,128]{1,0:T(8,128)S(1)} %get-tuple-element.11.density), custom_call_target="tpu_custom_call" | custom-call | tf_op jit(solution)/shard_map/sph_store/pallas_call | solution.py:471
